TPU v7x, 32 devices: a whole 2x2x4 slice. The times are simulated.
32 devices in a mesh: rep: 16 (over z, x, core), exp: 2 (over y).
Axes of the slice: x: 2, y: 2, z: 4, core: 2. Of those that a mesh axis runs over, the one named last changes fastest.
Arguments:
- hidden_states: bfloat16 [8192, 384], P(('rep', 'exp')), may hold values from -6 to 6
- expert_ids: int32 [8192, 2], P(('rep', 'exp')), may hold values from 0 to 7, all different within a row; in each aligned block of 256 rows (0 to 255, 256 to 511, ...) at most 96 rows name the same one
- router_weight: bfloat16 [384, 8], replicated, may hold values from -0.3125 to 0.3125
- up_weight: bfloat16 [8, 384, 2048], P('exp'), may hold values from -0.3125 to 0.3125
- down_weight: bfloat16 [8, 2048, 384], P('exp'), may hold values from -0.125 to 0.125
- projection: bfloat16 [384, 128], replicated, may hold values from -0.3125 to 0.3125
- teacher_scores: float32 [32, 32, 224], P(('rep', 'exp')), may hold values from -8 to 8
- query_lengths: int32 [32], P(('rep', 'exp')), may hold values from 8 to 32
- passage_lengths: int32 [32], P(('rep', 'exp')), may hold values from 56 to 224
Outputs:
- input_grad: bfloat16 [8192, 384], P(('rep', 'exp'))
- down_grad: float32 [8, 2048, 384], P('exp', 'rep')
- pair_kl: float32 [32], P(('rep', 'exp'))
Inputs may be any that keep to these rules, and one draw needn't show every extreme that they name: `expert_ids`: each row names 2 different experts. In the 256 rows of one device no expert is named more than 96 times, and in every draw some device names some expert exactly 96 times.
All inputs are finite; a program needn't handle non-finite values.
Results may differ from a plain program's by a relative error of at most 0.0086.
Values may be sent and summed in bfloat16 or wider, within the bound.
A program may use at most 64 MiB of HBM per device.

v0:
```python
import jax
import jax.numpy as jnp
from jax import lax
from jax.sharding import PartitionSpec as P

E = 8
TOP = 2
LQ = 32
LP = 224
CAP = 96


score_scale = 20.0
norm_eps = 1e-06
sqrt_half = 0.7071067811865476
density_scale = 0.3989422804014327


def gelu_value(preact):
    return 0.5 * preact * (1.0 + lax.erf(preact * sqrt_half))


def gelu_slope(preact):
    return (
        0.5 * (1.0 + lax.erf(preact * sqrt_half))
        + preact * jnp.exp(-0.5 * preact * preact) * density_scale
    )


def distill(vectors, teacher_scores, query_lengths, passage_lengths):
    queries = vectors[:, :LQ]
    passages = vectors[:, LQ:]
    scores = score_scale * jnp.einsum(
        "pqv,pkv->pqk", queries, passages, precision=lax.Precision.HIGHEST
    )
    query_mask = (jnp.arange(LQ, dtype=jnp.int32)[None, :] < query_lengths[:, None]).astype(
        jnp.float32
    )
    passage_mask = (jnp.arange(LP, dtype=jnp.int32)[None, :] < passage_lengths[:, None]).astype(
        jnp.float32
    )
    student_exp = jnp.exp(scores) * passage_mask[:, None, :]
    student_total = jnp.sum(student_exp, axis=-1, keepdims=True)
    student = student_exp / student_total
    log_student = scores - jnp.log(student_total)
    teacher_exp = jnp.exp(teacher_scores) * passage_mask[:, None, :]
    teacher_total = jnp.sum(teacher_exp, axis=-1, keepdims=True)
    teacher = teacher_exp / teacher_total
    log_teacher = teacher_scores - jnp.log(teacher_total)
    per_query = jnp.sum(teacher * (log_teacher - log_student), axis=-1)
    pair_kl = jnp.sum(per_query * query_mask, axis=-1)
    score_grad = (student - teacher) * query_mask[:, :, None]
    query_grad = score_scale * jnp.einsum(
        "pqk,pkv->pqv", score_grad, passages, precision=lax.Precision.HIGHEST
    )
    passage_grad = score_scale * jnp.einsum(
        "pqk,pqv->pkv", score_grad, queries, precision=lax.Precision.HIGHEST
    )
    return (pair_kl, jnp.concatenate([query_grad, passage_grad], axis=1))


def route_targets(expert_ids):
    flat_ids = expert_ids.reshape(-1)
    onehot = (flat_ids[:, None] == jnp.arange(E, dtype=jnp.int32)).astype(jnp.int32)
    earlier = jnp.cumsum(onehot, axis=0) - onehot
    return flat_ids * CAP + jnp.sum(earlier * onehot, axis=1)


def expert_pass(received, up_weight):
    local_experts = up_weight.shape[0]
    peer_count = received.shape[0] // local_experts
    grouped = received.reshape(peer_count, local_experts, received.shape[1], received.shape[2])
    preact = jnp.einsum("nekd,edf->nekf", grouped, up_weight, preferred_element_type=jnp.float32)
    hidden = gelu_value(preact).astype(jnp.bfloat16)
    return (preact, hidden)


def local(
    hidden_states,
    expert_ids,
    router_weight,
    up_weight,
    down_weight,
    projection,
    teacher_scores,
    query_lengths,
    passage_lengths,
):
    tok_rows, model_width = hidden_states.shape
    local_experts = up_weight.shape[0]
    targets = route_targets(expert_ids)
    logits = jnp.dot(hidden_states, router_weight, preferred_element_type=jnp.float32)
    choose = (expert_ids[..., None] == jnp.arange(E, dtype=jnp.int32)).astype(jnp.float32)
    picked = jnp.sum(logits[:, None, :] * choose, axis=-1)
    first_gate = jax.nn.sigmoid(picked[:, 0] - picked[:, 1])
    gate_values = jnp.stack([first_gate, 1.0 - first_gate], axis=1)
    routed = jnp.repeat(hidden_states, TOP, axis=0)
    send_rows = (
        jnp.zeros((E * CAP, model_width), jnp.bfloat16)
        .at[targets]
        .set(routed)
        .reshape(E, CAP, model_width)
    )
    received = lax.all_to_all(send_rows, "exp", split_axis=0, concat_axis=0, tiled=True)
    forward_preact, forward_hidden = expert_pass(received, up_weight)
    result = jnp.einsum(
        "nekf,efd->nekd", forward_hidden, down_weight, preferred_element_type=jnp.float32
    ).astype(jnp.bfloat16)
    returned = lax.all_to_all(
        result.reshape(received.shape), "exp", split_axis=0, concat_axis=0, tiled=True
    )
    returned_flat = returned.reshape(E * CAP, model_width)
    picked_out = returned_flat[targets].reshape(tok_rows, TOP, model_width)
    mixed_rows = (
        hidden_states.astype(jnp.float32)
        + jnp.sum(gate_values[:, :, None] * picked_out.astype(jnp.float32), axis=1)
    ).astype(jnp.bfloat16)
    projected = jnp.dot(mixed_rows, projection, preferred_element_type=jnp.float32)
    vec_norm = jnp.sqrt(jnp.sum(projected * projected, axis=-1, keepdims=True) + norm_eps)
    vectors = projected / vec_norm
    pairs_here = teacher_scores.shape[0]
    pair_kl, vector_grad = distill(
        vectors.reshape(pairs_here, -1, projected.shape[1]),
        teacher_scores,
        query_lengths,
        passage_lengths,
    )
    vector_grad = vector_grad.reshape(tok_rows, -1)
    radial = jnp.sum(vectors * vector_grad, axis=-1, keepdims=True)
    projected_grad = ((vector_grad - vectors * radial) / vec_norm).astype(jnp.bfloat16)
    mixed_grad = jnp.dot(projected_grad, projection.T, preferred_element_type=jnp.float32)
    out_grad = (gate_values[:, :, None] * mixed_grad[:, None, :]).astype(jnp.bfloat16)
    gate_grad = jnp.sum(mixed_grad[:, None, :] * picked_out.astype(jnp.float32), axis=-1)
    spread = (gate_grad[:, 0] - gate_grad[:, 1]) * gate_values[:, 0] * gate_values[:, 1]
    logit_grad = spread[:, None] * (choose[:, 0] - choose[:, 1])
    router_part = jnp.dot(
        logit_grad, router_weight.astype(jnp.float32).T, precision=lax.Precision.HIGHEST
    )
    grad_send = (
        jnp.zeros((E * CAP, model_width), jnp.bfloat16)
        .at[targets]
        .set(out_grad.reshape(-1, model_width))
        .reshape(E, CAP, model_width)
    )
    grad_received = lax.all_to_all(grad_send, "exp", split_axis=0, concat_axis=0, tiled=True)
    peer_count = grad_received.shape[0] // local_experts
    grad_grouped = grad_received.reshape(peer_count, local_experts, CAP, model_width)
    preact = forward_preact.reshape(received.shape[0], received.shape[1], -1).reshape(
        peer_count, local_experts, CAP, -1
    )
    hidden = forward_hidden.reshape(received.shape[0], received.shape[1], -1).reshape(
        peer_count, local_experts, CAP, -1
    )
    hidden_grad = jnp.einsum(
        "nekd,efd->nekf", grad_grouped, down_weight, preferred_element_type=jnp.float32
    )
    pre_grad = (hidden_grad * gelu_slope(preact)).astype(jnp.bfloat16)
    row_grad = jnp.einsum(
        "nekf,edf->nekd", pre_grad, up_weight, preferred_element_type=jnp.float32
    ).astype(jnp.bfloat16)
    returned_grad = lax.all_to_all(
        row_grad.reshape(grad_received.shape), "exp", split_axis=0, concat_axis=0, tiled=True
    )
    product_term = jnp.einsum(
        "nekf,nekd->efd", hidden, grad_grouped, preferred_element_type=jnp.float32
    )
    grad_shard = lax.psum_scatter(product_term, "rep", scatter_dimension=1, tiled=True)
    route_grad = returned_grad.reshape(E * CAP, model_width)[targets].reshape(
        tok_rows, TOP, model_width
    )
    input_grad = (
        mixed_grad + jnp.sum(route_grad.astype(jnp.float32), axis=1) + router_part
    ).astype(jnp.bfloat16)
    return (input_grad, grad_shard, pair_kl)


def solution(mesh):
    placed = (
        P(("rep", "exp"), None),
        P(("rep", "exp"), None),
        P(),
        P("exp", None, None),
        P("exp", None, None),
        P(),
        P(("rep", "exp"), None, None),
        P(("rep", "exp")),
        P(("rep", "exp")),
    )
    return jax.shard_map(
        local,
        mesh=mesh,
        in_specs=placed,
        out_specs=(P(("rep", "exp"), None), P("exp", "rep", None), P(("rep", "exp"))),
        check_vma=False,
    )
```

profile of v0, /device:TPU:0, one launch (start us, length us, event | category | flops | bytes accessed | tf_op | source)
XLA Modules:
  0.0 233.2 jit_solution(7241854240606519401)
XLA Ops:
  7.2 0.0 copy-start
  7.2 0.7 broadcast_multiply_fusion
  7.9 0.8 copy.51
  8.7 0.1 eq.45
  8.9 0.1 eq.41
  9.0 0.1 copy.50
  9.1 0.1 mul.190
  9.3 1.1 reduce-window.6
  10.5 0.2 slice_reduce_fusion
  10.7 1.1 broadcast_in_dim.2
  11.9 0.1 reshape.236
  12.0 0.1 fusion.71
  12.1 3.2 %scatter_custom_fusion = bf16[768,384]{1,0:T(8,128)(2,1)} fusion(s32[512]{0:T(512)S(1)} %bitcast.159, bf16[512,384]{1,0:T(8,128)(2,1)S(1)} %reshape.236, bf16[]{:T(256)} %constant.14.clone.1), kind=kCustom, calls=%fused_computation.50 | custom fusion | bytes 589826 | tf_op jit(solution)/shard_map/scatter | solution.py:101
  15.3 4.3 %all-to-all-start = ((bf16[8,96,384]{2,1,0:T(8,128)(2,1)}), bf16[8,96,384]{2,1,0:T(8,128)(2,1)S(1)}, u32[]{:S(2)}, u32[]{:S(2)}) async-start(bf16[8,96,384]{2,1,0:T(8,128)(2,1)} %bitcast.4), calls=%async_computation | async-start | bytes 1179648 | tf_op jit(solution)/shard_map/all_to_all | solution.py:104
  19.6 1.0 fusion.90
  20.6 0.8 select_reduce_fusion
  22.7 0.1 copy.49
  22.9 0.0 copy-start.8
  22.9 0.1 mul.214
  23.0 6.0 %all-to-all-done = bf16[8,96,384]{2,1,0:T(8,128)(2,1)S(1)} async-done(((bf16[8,96,384]{2,1,0:T(8,128)(2,1)}), bf16[8,96,384]{2,1,0:T(8,128)(2,1)S(1)}, u32[]{:S(2)}, u32[]{:S(2)}) %all-to-all-start) | async-done | bytes 589856 | tf_op jit(solution)/shard_map/all_to_all | solution.py:104
  29.0 0.8 copy-done.6
  29.8 6.0 %fusion.15 = (bf16[2,4,96,2048]{3,2,0,1:T(8,128)(2,1)S(1)}, f32[4,2,96,2048]{3,2,1,0:T(8,128)}) fusion(bf16[4,384,2048]{2,1,0:T(8,128)(2,1)} %param.12, bf16[2,4,96,384]{3,2,1,0:T(8,128)(2,1)} %bitcast.156), kind=kOutput, calls=%fused_computation.22 | convolution fusion | flops 1215823872 | bytes 16318464 | tf_op jit(solution)/shard_map/nekd,edf->nekf/dot_general | solution.py:73
  35.8 4.6 %fusion.36 = bf16[2,4,96,384]{3,2,0,1:T(8,128)(2,1)S(1)} fusion(bf16[2,4,96,2048]{3,2,0,1:T(8,128)(2,1)S(1)} %get-tuple-element.7, bf16[4,2048,384]{2,1,0:T(8,128)(2,1)} %param.13), kind=kOutput, calls=%fused_computation.31 | convolution fusion | flops 1208254464 | bytes 10027008 | tf_op jit(solution)/shard_map/nekf,efd->nekd/dot_general | solution.py:106
  40.4 0.9 copy.54
  41.3 4.2 %all-to-all-start.1 = ((bf16[8,96,384]{2,1,0:T(8,128)(2,1)}), bf16[8,96,384]{2,1,0:T(8,128)(2,1)}, u32[]{:S(2)}, u32[]{:S(2)}) async-start(bf16[8,96,384]{2,1,0:T(8,128)(2,1)} %bitcast.157), calls=%async_computation.1 | async-start | bytes 1179648 | tf_op jit(solution)/shard_map/all_to_all | solution.py:109
  45.5 0.2 reduce-scatter.2.cloned.1.call-start
  45.8 0.1 fusion.69
  45.9 8.1 %all-to-all-done.1 = bf16[8,96,384]{2,1,0:T(8,128)(2,1)} async-done(((bf16[8,96,384]{2,1,0:T(8,128)(2,1)}), bf16[8,96,384]{2,1,0:T(8,128)(2,1)}, u32[]{:S(2)}, u32[]{:S(2)}) %all-to-all-start.1) | async-done | bytes 589856 | tf_op jit(solution)/shard_map/all_to_all | solution.py:109
  54.0 3.6 %gather_fusion = bf16[512,384]{1,0:T(8,128)(2,1)} fusion(bf16[768,384]{1,0:T(8,128)(2,1)} %bitcast.13, s32[1024]{0:T(1024)S(1)} %pad_clamp_fusion), kind=kCustom, calls=%fused_computation | custom fusion | bytes 788480 | tf_op jit(solution)/shard_map/gather | solution.py:113
  57.6 2.3 reshape.214
  59.8 2.2 multiply_reduce_fusion.1
  62.0 0.3 multiply_reduce_fusion.3
  62.3 0.1 fusion.87
  62.5 0.4 fusion.67
  62.9 0.3 fusion.48
  63.2 0.4 fusion.47
  63.6 0.2 multiply_reduce_fusion.2
  63.8 0.3 fusion.59
  64.1 0.8 copy-done.2
  64.9 1.1 mul.216
  66.0 2.5 %mul.217 = f32[512,384]{1,0:T(8,128)} reshape(f32[256,2,384]{2,1,0:T(2,128)} %mul.216) | data formatting | bytes 1572864 | tf_op jit(solution)/shard_map/mul | solution.py:132
  68.6 3.8 %scatter_custom_fusion.1 = bf16[768,384]{1,0:T(8,128)(2,1)} fusion(s32[512]{0:T(512)S(1)} %bitcast.161, f32[512,384]{1,0:T(8,128)} %mul.217, f32[512]{0:T(512)S(1)} %mul.214, bf16[]{:T(256)} %constant.14.clone.1), kind=kCustom, calls=%fused_computation.46 | custom fusion | flops 393216 | bytes 1378306 | tf_op jit(solution)/shard_map/scatter | solution.py:142
  72.4 11.0 %all_to_all.20 = bf16[8,96,384]{2,1,0:T(8,128)(2,1)S(1)} all-to-all(bf16[8,96,384]{2,1,0:T(8,128)(2,1)} %bitcast.158), channel_id=1, replica_groups=mesh['rep'=16,'exp'=2] {'exp'}, dimensions={0} | all-to-all | bytes 1179648 | tf_op jit(solution)/shard_map/all_to_all | solution.py:145
  83.5 0.8 copy-done.4
  84.3 7.0 %convolution_bitcast_fusion = f32[4,2048,384]{2,1,0:T(8,128)} fusion(bf16[2,4,96,2048]{3,2,0,1:T(8,128)(2,1)S(1)} %get-tuple-element.7, bf16[2,4,96,384]{3,2,1,0:T(8,128)(2,1)S(1)} %bitcast.154), kind=kOutput, calls=%fused_computation.25 | convolution fusion | flops 1207959552 | bytes 16318464 | tf_op jit(solution)/shard_map/nekf,nekd->efd/dot_general | solution.py:164
  91.3 0.0 reduce-scatter.2.cloned.1.call-update
  91.3 0.6 copy-done.10
  92.0 0.5 copy-done.1
  92.4 0.1 copy-done.3
  92.5 0.5 multiply_reduce_fusion
  93.1 0.1 fusion.89
  93.2 0.1 copy.65
  93.2 0.1 copy.64
  93.3 0.2 fusion.63
  93.5 10.4 %fusion.39 = bf16[2,4,96,384]{3,2,0,1:T(8,128)(2,1)S(1)} fusion(bf16[4,384,2048]{2,1,0:T(8,128)(2,1)} %param.12, f32[4,2,96,2048]{3,2,1,0:T(8,128)} %get-tuple-element.8, bf16[4,2048,384]{2,1,0:T(8,128)(2,1)} %param.13, bf16[2,4,96,384]{3,2,1,0:T(8,128)(2,1)S(1)} %bitcast.155), kind=kOutput, calls=%fused_computation.32 | convolution fusion | flops 2431942656 | bytes 20054016 | tf_op jit(solution)/shard_map/nekf,edf->nekd/dot_general | solution.py:158
  103.9 0.9 copy.57
  104.8 3.7 %all-to-all-start.3 = ((bf16[8,96,384]{2,1,0:T(8,128)(2,1)}), bf16[8,96,384]{2,1,0:T(8,128)(2,1)S(1)}, u32[]{:S(2)}, u32[]{:S(2)}) async-start(bf16[8,96,384]{2,1,0:T(8,128)(2,1)} %bitcast.30), calls=%async_computation.3 | async-start | bytes 1179648 | tf_op jit(solution)/shard_map/all_to_all | solution.py:161
  108.6 0.6 fusion.80
  109.2 6.1 %all-to-all-done.3 = bf16[8,96,384]{2,1,0:T(8,128)(2,1)S(1)} async-done(((bf16[8,96,384]{2,1,0:T(8,128)(2,1)}), bf16[8,96,384]{2,1,0:T(8,128)(2,1)S(1)}, u32[]{:S(2)}, u32[]{:S(2)}) %all-to-all-start.3) | async-done | bytes 589856 | tf_op jit(solution)/shard_map/all_to_all | solution.py:161
  115.3 1.9 gather_fusion.1
  117.2 0.4 reshape.215
  117.6 0.9 reduce_sum.111
  118.6 1.1 fusion.46
  119.6 106.7 %reduce-scatter.2.cloned.1.call-done = f32[4,128,384]{2,1,0:T(8,128)} async-done(((f32[4,2048,384]{2,1,0:T(8,128)}), f32[4,128,384]{2,1,0:T(8,128)}) %reduce-scatter.2.cloned.1.call-update) | async-done | bytes 786448 | tf_op jit(solution)/shard_map/reduce_scatter | solution.py:167
  (30 shorter events, 0.2 us)
Async XLA Ops:
  7.2 54.8 %copy-start = (bf16[384,128]{1,0:T(8,128)(2,1)S(1)}, bf16[384,128]{1,0:T(8,128)(2,1)}, u32[]{:S(2)}) copy-start(bf16[384,128]{1,0:T(8,128)(2,1)} %param.14) | copy-start | bytes 294916
  15.3 13.7 %all-to-all-start = ((bf16[8,96,384]{2,1,0:T(8,128)(2,1)}), bf16[8,96,384]{2,1,0:T(8,128)(2,1)S(1)}, u32[]{:S(2)}, u32[]{:S(2)}) async-start(bf16[8,96,384]{2,1,0:T(8,128)(2,1)} %bitcast.4), calls=%async_computation | async-start | bytes 1179648 | tf_op jit(solution)/shard_map/all_to_all | solution.py:104
  22.9 6.2 %copy-start.8 = (f32[256,2]{1,0:T(8,128)}, f32[256,2]{1,0:T(8,128)S(1)}, u32[]{:S(2)}) copy-start(f32[256,2]{1,0:T(8,128)S(1)} %copy.49) | copy-start | bytes 6148
  29.0 0.8 copy-start.6
  35.8 10.0 %copy-start.9 = (f32[1,32,224]{2,1,0:T(8,128)S(1)}, f32[1,32,224]{2,1,0:T(8,128)}, u32[]{:S(2)}) copy-start(f32[1,32,224]{2,1,0:T(8,128)} %param.15) | copy-start | bytes 86020
  40.4 21.6 %copy-start.7 = (bf16[256,384]{1,0:T(8,128)(2,1)S(1)}, bf16[256,384]{1,0:T(8,128)(2,1)}, u32[]{:S(2)}) copy-start(bf16[256,384]{1,0:T(8,128)(2,1)} %param.9) | copy-start | bytes 589828
  41.3 12.7 %all-to-all-start.1 = ((bf16[8,96,384]{2,1,0:T(8,128)(2,1)}), bf16[8,96,384]{2,1,0:T(8,128)(2,1)}, u32[]{:S(2)}, u32[]{:S(2)}) async-start(bf16[8,96,384]{2,1,0:T(8,128)(2,1)} %bitcast.157), calls=%async_computation.1 | async-start | bytes 1179648 | tf_op jit(solution)/shard_map/all_to_all | solution.py:109
  45.5 180.9 %reduce-scatter.2.cloned.1.call-start = ((), (), s32[]{:S(2)}) async-start(), calls=%async_computation.5 | async-start | bytes 13369344 | tf_op jit(solution)/shard_map/reduce_scatter | solution.py:167
  64.1 0.8 copy-start.2
  83.5 0.8 copy-start.4
  91.3 0.7 copy-start.10
  91.3 1.1 copy-start.1
  91.3 1.2 copy-start.3
  91.3 2.2 copy-start.5
  103.9 14.6 %copy-start.11 = (bf16[384,8]{0,1:T(8,128)(2,1)S(1)}, bf16[384,8]{0,1:T(8,128)(2,1)}, u32[]{:S(2)}) copy-start(bf16[384,8]{0,1:T(8,128)(2,1)} %param.11) | copy-start | bytes 18436
  104.8 10.4 %all-to-all-start.3 = ((bf16[8,96,384]{2,1,0:T(8,128)(2,1)}), bf16[8,96,384]{2,1,0:T(8,128)(2,1)S(1)}, u32[]{:S(2)}, u32[]{:S(2)}) async-start(bf16[8,96,384]{2,1,0:T(8,128)(2,1)} %bitcast.30), calls=%async_computation.3 | async-start | bytes 1179648 | tf_op jit(solution)/shard_map/all_to_all | solution.py:161
Sparse Core Ops, SparseCore 0:
  91.5 134.8 reduce-scatter.1
where the time goes:
time: 234 us; the launch traced here: 233 us
  waiting for transfers between devices  127 us (54%)
  matrix products  31.8 us (14%)
  local copies, waits for them, and re-layouts  23.9 us (10%)
  between operations  15.6 us (7%)
  starting transfers between devices  12.4 us (5%)
  other arithmetic  11.5 us (5%)
  blocking collectives  11 us (5%)
    reduce_scatter x1, waiting for transfers between devices, local(): lax.psum_scatter(product_term, 'rep', scatter_dimension=1, tiled=True)  107 us
    all_to_all x1, blocking collectives, local(): lax.all_to_all(grad_send, 'exp', split_axis=0, concat_axis=0, tiled=True)  11 us
    dot_general x1, matrix products, local(): jnp.einsum('nekf,edf->nekd', pre_grad, up_weight, preferred_element_type=...  10.4 us
    all_to_all x1, waiting for transfers between devices, local(): lax.all_to_all(result.reshape(received.shape), 'exp', split_axis=0, conca...  8.09 us
    dot_general x1, matrix products, local(): jnp.einsum('nekf,nekd->efd', hidden, grad_grouped, preferred_element_type...  7.03 us
    all_to_all x1, waiting for transfers between devices, local(): lax.all_to_all(row_grad.reshape(grad_received.shape), 'exp', split_axis=0...  6.09 us
    all_to_all x1, waiting for transfers between devices, local(): lax.all_to_all(send_rows, 'exp', split_axis=0, concat_axis=0, tiled=True)  5.99 us
    dot_general x1, matrix products, expert_pass(): jnp.einsum('nekd,edf->nekf', grouped, up_weight, preferred_element_type=j...  5.95 us
  transfers between devices with their start and end apart: 4, of which 4 were waited for; matrix products, arithmetic and copies ran while one was open for 8% of the time, Pallas kernels for 0%

commit v1 on v0

v1 whole, which is shorter than its diff:
```python
import jax
import jax.numpy as jnp
from jax import lax
from jax.sharding import PartitionSpec as P

E = 8
LQ = 32
LP = 224
CAP = 96


score_scale = 20.0
norm_eps = 1e-06
sqrt_half = 0.7071067811865476
density_scale = 0.3989422804014327


def gelu_value(preact):
    return 0.5 * preact * (1.0 + lax.erf(preact * sqrt_half))


def gelu_slope(preact):
    return (
        0.5 * (1.0 + lax.erf(preact * sqrt_half))
        + preact * jnp.exp(-0.5 * preact * preact) * density_scale
    )


def distill(vectors, teacher_scores, query_lengths, passage_lengths):
    queries = vectors[:, :LQ]
    passages = vectors[:, LQ:]
    scores = score_scale * jnp.einsum(
        "pqv,pkv->pqk", queries, passages, precision=lax.Precision.HIGHEST
    )
    query_mask = (jnp.arange(LQ, dtype=jnp.int32)[None, :] < query_lengths[:, None]).astype(
        jnp.float32
    )
    passage_mask = (jnp.arange(LP, dtype=jnp.int32)[None, :] < passage_lengths[:, None]).astype(
        jnp.float32
    )
    student_exp = jnp.exp(scores) * passage_mask[:, None, :]
    student_total = jnp.sum(student_exp, axis=-1, keepdims=True)
    student = student_exp / student_total
    log_student = scores - jnp.log(student_total)
    teacher_exp = jnp.exp(teacher_scores) * passage_mask[:, None, :]
    teacher_total = jnp.sum(teacher_exp, axis=-1, keepdims=True)
    teacher = teacher_exp / teacher_total
    log_teacher = teacher_scores - jnp.log(teacher_total)
    per_query = jnp.sum(teacher * (log_teacher - log_student), axis=-1)
    pair_kl = jnp.sum(per_query * query_mask, axis=-1)
    score_grad = (student - teacher) * query_mask[:, :, None]
    query_grad = score_scale * jnp.einsum(
        "pqk,pkv->pqv", score_grad, passages, precision=lax.Precision.HIGHEST
    )
    passage_grad = score_scale * jnp.einsum(
        "pqk,pqv->pkv", score_grad, queries, precision=lax.Precision.HIGHEST
    )
    return (pair_kl, jnp.concatenate([query_grad, passage_grad], axis=1))


def fetch(block, shift):
    size = lax.axis_size("exp")
    return lax.ppermute(block, "exp", [(i, (i - shift) % size) for i in range(size)])


def give_back(block, shift):
    size = lax.axis_size("exp")
    return lax.ppermute(block, "exp", [(i, (i + shift) % size) for i in range(size)])


def spread_out(block):
    size = lax.axis_size("exp")
    return jnp.stack([block] + [fetch(block, shift) for shift in range(1, size)])


def bring_home(parts):
    total = parts[0]
    for shift in range(1, parts.shape[0]):
        total = total + give_back(parts[shift].astype(jnp.bfloat16), shift).astype(jnp.float32)
    return total


def scatter_sum(terms):
    return lax.psum_scatter(
        terms.astype(jnp.bfloat16), "rep", scatter_dimension=1, tiled=True
    ).astype(jnp.float32)


def local(
    hidden_states,
    expert_ids,
    router_weight,
    up_weight,
    down_weight,
    projection,
    teacher_scores,
    query_lengths,
    passage_lengths,
):
    tok_rows, width = hidden_states.shape
    here = up_weight.shape[0]
    first = lax.axis_index("exp") * here
    rows = spread_out(hidden_states)
    ids = spread_out(expert_ids.T)
    blocks = rows.shape[0]
    names = jnp.arange(E, dtype=jnp.int32)[None, :, None]
    is_first = (ids[:, :1] == names).astype(jnp.float32)
    is_second = (ids[:, 1:] == names).astype(jnp.float32)
    logits = jnp.einsum("de,ntd->net", router_weight, rows, preferred_element_type=jnp.float32)
    side = is_first - is_second
    first_gate = jax.nn.sigmoid(jnp.sum(logits * side, axis=1, keepdims=True))
    second_gate = 1.0 - first_gate
    named = is_first + is_second
    before = jnp.arange(tok_rows)[:, None] < jnp.arange(tok_rows)[None, :]
    slots = jnp.einsum(
        "net,tu->neu",
        named.astype(jnp.bfloat16),
        before.astype(jnp.bfloat16),
        preferred_element_type=jnp.float32,
    ).astype(jnp.int32)
    slots = jnp.where(named > 0, slots, -1)
    mine = lambda value: lax.dynamic_slice_in_dim(value, first, here, axis=1)
    slots_here = mine(slots)
    gates_here = mine(is_first * first_gate + is_second * second_gate)
    side_here = mine(side)
    hit = slots_here[:, :, None, :] == jnp.arange(CAP, dtype=jnp.int32)[None, None, :, None]
    pick = hit.astype(jnp.bfloat16)
    row_gate = jnp.sum(jnp.where(hit, gates_here[:, :, None, :], 0.0), axis=-1)
    row_gate = row_gate.transpose(1, 0, 2).reshape(here, blocks * CAP, 1)

    def to_slots(tokens):
        picked = jnp.einsum("nect,ntd->encd", pick, tokens, preferred_element_type=jnp.float32)
        return picked.astype(jnp.bfloat16).reshape(here, blocks * CAP, width)

    def to_tokens(slot_rows):
        return jnp.einsum(
            "nect,encd->ntd",
            pick,
            slot_rows.reshape(here, blocks, CAP, width),
            preferred_element_type=jnp.float32,
        )

    expert_rows = to_slots(rows)
    preact = jnp.einsum(
        "erd,edf->erf", expert_rows, up_weight, preferred_element_type=jnp.float32
    )
    hidden = gelu_value(preact).astype(jnp.bfloat16)
    out = jnp.einsum("erf,efd->erd", hidden, down_weight, preferred_element_type=jnp.float32)
    mixed = bring_home(to_tokens((row_gate * out).astype(jnp.bfloat16)))
    mixed_rows = (hidden_states.astype(jnp.float32) + mixed).astype(jnp.bfloat16)
    projected = jnp.dot(mixed_rows, projection, preferred_element_type=jnp.float32)
    vec_norm = jnp.sqrt(jnp.sum(projected * projected, axis=-1, keepdims=True) + norm_eps)
    vectors = projected / vec_norm
    pairs_here = teacher_scores.shape[0]
    pair_kl, vector_grad = distill(
        vectors.reshape(pairs_here, -1, projected.shape[1]),
        teacher_scores,
        query_lengths,
        passage_lengths,
    )
    vector_grad = vector_grad.reshape(tok_rows, -1)
    radial = jnp.sum(vectors * vector_grad, axis=-1, keepdims=True)
    projected_grad = ((vector_grad - vectors * radial) / vec_norm).astype(jnp.bfloat16)
    mixed_grad = jnp.dot(projected_grad, projection.T, preferred_element_type=jnp.float32)
    grad_rows = to_slots(spread_out(mixed_grad.astype(jnp.bfloat16))).astype(jnp.float32)
    out_grad = (row_gate * grad_rows).astype(jnp.bfloat16)
    product = jnp.einsum("erf,erd->efd", hidden, out_grad, preferred_element_type=jnp.float32)
    down_grad = scatter_sum(product)
    gate_grad = jnp.sum(grad_rows * out, axis=-1).reshape(here, blocks, CAP).transpose(1, 0, 2)
    hit_grad = jnp.sum(jnp.where(hit, gate_grad[..., None], 0.0), axis=2)
    spread = jnp.sum(hit_grad * side_here, axis=1, keepdims=True) * first_gate * second_gate
    router_part = jnp.einsum(
        "net,de->ntd",
        spread * side,
        router_weight.astype(jnp.float32),
        precision=lax.Precision.HIGHEST,
    )
    hidden_grad = jnp.einsum(
        "erd,efd->erf", out_grad, down_weight, preferred_element_type=jnp.float32
    )
    pre_grad = (hidden_grad * gelu_slope(preact)).astype(jnp.bfloat16)
    row_grad = jnp.einsum(
        "erf,edf->erd", pre_grad, up_weight, preferred_element_type=jnp.float32
    ).astype(jnp.bfloat16)
    input_grad = (mixed_grad + bring_home(to_tokens(row_grad) + router_part)).astype(jnp.bfloat16)
    return (input_grad, down_grad, pair_kl)


def solution(mesh):
    placed = (
        P(("rep", "exp"), None),
        P(("rep", "exp"), None),
        P(),
        P("exp", None, None),
        P("exp", None, None),
        P(),
        P(("rep", "exp"), None, None),
        P(("rep", "exp")),
        P(("rep", "exp")),
    )
    return jax.shard_map(
        local,
        mesh=mesh,
        in_specs=placed,
        out_specs=(P(("rep", "exp"), None), P("exp", "rep", None), P(("rep", "exp"))),
        check_vma=False,
    )
```

time: 234 us -> 142 us (0.61)
  waiting for transfers between devices: 127 us -> 87.2 us
  local copies, waits for them, and re-layouts: 23.9 us -> 0.42 us
  blocking collectives: 11 us -> 0 us
  starting transfers between devices: 12.4 us -> 4.52 us
  other arithmetic: 11.5 us -> 5.41 us
  matrix products: 31.8 us -> 28.5 us
    reduce_scatter x1, waiting for transfers between devices: 107 us -> 68.1 us  [scatter_sum(): lax.psum_scatter(terms.astype(jnp.bfloat16), 'rep', scatter_dimension=1,...]
    all_to_all x3 -> x0, waiting for transfers between devices: 20.2 us -> none  [the longest x1 8.09 us: local(): lax.all_to_all(result.reshape(received.shape), 'exp', split_axis=0, conca...]
    ppermute x0 -> x5, waiting for transfers between devices: none -> 19.1 us  [the longest x2 9.79 us: give_back(): lax.ppermute(block, 'exp', [(i, (i + shift) % size) for i in range(size)])]
    all_to_all x3 -> x0, starting transfers between devices: 12.2 us -> none  [the longest x1 4.26 us: local(): lax.all_to_all(send_rows, 'exp', split_axis=0, concat_axis=0, tiled=True)]
    all_to_all x1 -> x0, blocking collectives: 11 us -> none  [local(): lax.all_to_all(grad_send, 'exp', split_axis=0, concat_axis=0, tiled=True)]
    gather x2 -> x0, local copies, waits for them, and re-layouts: 5.51 us -> none  [the longest x1 3.58 us: local(): picked_out = returned_flat[targets].reshape(tok_rows, TOP, model_width)]
    unnamed x27 -> x13, local copies, waits for them, and re-layouts: 4.6 us -> 0.05 us
    ppermute x0 -> x5, starting transfers between devices: none -> 4.48 us  [the longest x3 3.73 us: fetch(): lax.ppermute(block, 'exp', [(i, (i - shift) % size) for i in range(size)])]
  transfers between devices with their start and end apart: 4 -> 6, of which waited for: 4 -> 6; matrix products, arithmetic and copies ran while one was open for 8% -> 10% of each run, Pallas kernels for 0% -> 0%
where the time goes in v1:
time: 142 us
  waiting for transfers between devices  87.2 us (61%)
  matrix products  28.5 us (20%)
  between operations  15.6 us (11%)
  other arithmetic  5.41 us (4%)
  starting transfers between devices  4.52 us (3%)
    reduce_scatter x1, waiting for transfers between devices, scatter_sum(): lax.psum_scatter(terms.astype(jnp.bfloat16), 'rep', scatter_dimension=1,...  68.1 us
    ppermute x2, waiting for transfers between devices, give_back(): lax.ppermute(block, 'exp', [(i, (i + shift) % size) for i in range(size)])  9.79 us
    dot_general x1, matrix products, local(): jnp.einsum('erf,edf->erd', pre_grad, up_weight, preferred_element_type=jn...  9.36 us
    ppermute x3, waiting for transfers between devices, fetch(): lax.ppermute(block, 'exp', [(i, (i - shift) % size) for i in range(size)])  9.35 us
    dot_general x1, matrix products, local(): jnp.einsum('erd,edf->erf', expert_rows, up_weight, preferred_element_type...  5.92 us
    dot_general x1, matrix products, local(): jnp.einsum('erf,erd->efd', hidden, out_grad, preferred_element_type=jnp.f...  5.14 us
    ppermute x3, starting transfers between devices, fetch(): lax.ppermute(block, 'exp', [(i, (i - shift) % size) for i in range(size)])  3.73 us
  transfers between devices with their start and end apart: 6, of which 6 were waited for; matrix products, arithmetic and copies ran while one was open for 10% of the time, Pallas kernels for 0%

profile of v1, /device:TPU:0, one launch (start us, length us, event | category | flops | bytes accessed | tf_op | source)
XLA Modules:
  0.0 141.7 jit_solution(781971131841259376)
XLA Ops:
  7.2 0.0 copy-start
  7.2 0.0 reduce-scatter.2.cloned.1.call-start
  7.2 3.1 %collective-permute-start = (s32[2,256]{1,0:T(2,128)}, s32[2,256]{1,0:T(2,128)S(1)}, u32[]{:S(2)}, u32[]{:S(2)}) collective-permute-start(s32[2,256]{1,0:T(2,128)} %bitcast.151), channel_id=1, source_target_pairs={{0,1},{1,0},{2,3},{3,2},{4,5},{5,4},{6,7},{7,6},{8,9},{9,8},{10,11... | collective-permute-start | bytes 6152 | tf_op jit(solution)/shard_map/ppermute | solution.py:63
  10.3 0.1 collective-permute-start.1
  11.7 0.4 collective-permute-done
  12.1 0.8 fusion.56
  12.8 0.1 fusion.31
  13.0 3.8 %collective-permute-done.1 = bf16[256,384]{1,0:T(8,128)(2,1)S(1)} collective-permute-done((bf16[256,384]{1,0:T(8,128)(2,1)}, bf16[256,384]{1,0:T(8,128)(2,1)S(1)}, u32[]{:S(2)}, u32[]{:S(2)}) %collective-permute-start.1) | collective-permute-done | bytes 196640 | tf_op jit(solution)/shard_map/ppermute | solution.py:63
  16.9 1.2 fusion.14
  18.0 1.3 fusion.10
  19.4 0.2 select_reduce_fusion.1
  19.6 0.1 mul.178
  19.7 0.0 slice-start
  19.7 0.1 copy.26
  19.8 0.0 slice-start.1
  19.8 5.9 %multiply_convert_fusion = (bf16[4,192,2048]{2,1,0:T(8,128)(2,1)S(1)}, f32[4,192,2048]{2,1,0:T(8,128)}) fusion(bf16[4,192,384]{2,1,0:T(8,128)(2,1)S(1)} %bitcast.143, bf16[4,384,2048]{2,1,0:T(8,128)(2,1)} %param.12), kind=kOutput, calls=%fused_computation.7 | convolution fusion | flops 1215823872 | bytes 16318464 | tf_op jit(solution)/shard_map/erd,edf->erf/dot_general | solution.py:144
  25.7 0.0 slice-done
  25.7 0.0 slice-done.1
  25.7 0.0 copy-start.2
  25.7 0.0 copy-start.1
  25.7 1.9 %multiply_convert_fusion.2 = (bf16[4,192,384]{2,1,0:T(8,128)(2,1)S(1)}, f32[4,192,384]{2,1,0:T(8,128)S(1)}) fusion(f32[4,192]{1,0:T(4,128)S(1)} %mul.178, bf16[4,192,2048]{2,1,0:T(8,128)(2,1)S(1)} %get-tuple-element.9, bf16[4,2048,384]{2,1,0:T(8,128)(2,1)S(1)} %bitcast.142), kind=kOutput, calls=%fused_computation.22 | convolution fusion | flops 1208549376 | bytes 11209728 | tf_op jit(solution)/shard_map/erf,efd->erd/dot_general | solution.py:148
  27.6 0.5 convolution_bitcast_fusion.1
  28.1 0.4 collective-permute-start.2
  28.6 0.0 copy-done.2
  28.6 0.1 fusion.47
  28.7 5.2 %collective-permute-done.2 = bf16[256,384]{1,0:T(8,128)(2,1)S(1)} collective-permute-done((bf16[256,384]{1,0:T(8,128)(2,1)S(1)}, bf16[256,384]{1,0:T(8,128)(2,1)S(1)}, u32[]{:S(2)}, u32[]{:S(2)}) %collective-permute-start.2) | collective-permute-done | bytes 196640 | tf_op jit(solution)/shard_map/ppermute | solution.py:68
  33.9 0.0 copy-done
  33.9 0.0 copy-done.1
  33.9 0.3 multiply_reduce_fusion.2
  34.2 0.1 fusion.67
  34.3 0.4 fusion.45
  34.7 0.3 fusion.13
  35.0 0.4 fusion.11
  35.5 0.2 multiply_reduce_fusion.1
  35.7 0.3 fusion.68
  36.0 0.6 collective-permute-start.3
  36.6 5.1 %collective-permute-done.3 = bf16[256,384]{1,0:T(8,128)(2,1)S(1)} collective-permute-done((bf16[256,384]{1,0:T(8,128)(2,1)S(1)}, bf16[256,384]{1,0:T(8,128)(2,1)S(1)}, u32[]{:S(2)}, u32[]{:S(2)}) %collective-permute-start.3) | collective-permute-done | bytes 196640 | tf_op jit(solution)/shard_map/ppermute | solution.py:63
  41.7 0.4 fusion.9
  42.1 0.1 copy.28
  42.2 5.1 %convolution_convert_fusion = bf16[4,2048,384]{2,1,0:T(8,128)(2,1)} fusion(bf16[4,192,2048]{2,1,0:T(8,128)(2,1)S(1)} %get-tuple-element.9, f32[4,192,384]{2,1,0:T(8,128)S(1)} %bitcast.138, f32[4,192]{1,0:T(4,128)S(1)} %mul.178), kind=kOutput, calls=%fused_computation.9 | convolution fusion | flops 1211695104 | bytes 10619904 | tf_op jit(solution)/shard_map/erf,erd->efd/dot_general | solution.py:167
  47.3 0.0 reduce-scatter.2.cloned.1.call-update
  47.3 0.2 multiply_reduce_fusion
  47.6 0.1 reshape.154
  47.7 0.2 select_reduce_fusion
  47.9 0.0 copy-start.3
  47.9 9.4 %fusion.7 = bf16[4,192,384]{2,1,0:T(8,128)(2,1)S(1)} fusion(bf16[4,384,2048]{2,1,0:T(8,128)(2,1)} %param.12, f32[4,192,2048]{2,1,0:T(8,128)} %get-tuple-element.10, bf16[4,2048,384]{2,1,0:T(8,128)(2,1)} %param.13, f32[4,192,384]{2,1,0:T(8,128)S(1)} %bitcast.140, f32[4,192]{1,0:T(4,128)S(1)} %mul.178), kind=kOutput, calls=%fused_computation.11 | convolution fusion | flops 2432532480 | bytes 20646912 | tf_op jit(solution)/shard_map/erf,edf->erd/dot_general | solution.py:182
  57.3 0.5 convolution_bitcast_fusion
  57.7 0.0 copy-done.3
  57.8 0.5 convolution_add_fusion
  58.3 0.3 collective-permute-start.4
  58.6 0.2 fusion.41
  58.8 0.6 fusion.57
  59.4 4.6 %collective-permute-done.4 = bf16[256,384]{1,0:T(8,128)(2,1)S(1)} collective-permute-done((bf16[256,384]{1,0:T(8,128)(2,1)S(1)}, bf16[256,384]{1,0:T(8,128)(2,1)S(1)}, u32[]{:S(2)}, u32[]{:S(2)}) %collective-permute-start.4) | collective-permute-done | bytes 196640 | tf_op jit(solution)/shard_map/ppermute | solution.py:68
  64.1 0.8 fusion.19
  64.8 68.1 %reduce-scatter.2.cloned.1.call-done = bf16[4,128,384]{2,1,0:T(8,128)(2,1)} async-done(((bf16[4,2048,384]{2,1,0:T(8,128)(2,1)}), bf16[4,128,384]{2,1,0:T(8,128)(2,1)}) %reduce-scatter.2.cloned.1.call-update) | async-done | bytes 393232 | tf_op jit(solution)/shard_map/reduce_scatter | solution.py:84
  132.9 1.9 %convert_element_type.129 = f32[4,128,384]{2,1,0:T(8,128)} convert(bf16[4,128,384]{2,1,0:T(8,128)(2,1)} %reduce-scatter.2.cloned.1.call-done) | non-fusion elementwise | flops 196608 | bytes 1179648 | tf_op jit(solution)/shard_map/convert_element_type | solution.py:86
  (19 shorter events, 0.2 us)
Async XLA Ops:
  7.2 26.7 %copy-start = (bf16[384,128]{1,0:T(8,128)(2,1)S(1)}, bf16[384,128]{1,0:T(8,128)(2,1)}, u32[]{:S(2)}) copy-start(bf16[384,128]{1,0:T(8,128)(2,1)} %param.14) | copy-start | bytes 294916
  7.2 125.7 %reduce-scatter.2.cloned.1.call-start = ((), (), s32[]{:S(2)}) async-start(), calls=%async_computation.1 | async-start | bytes 6684672 | tf_op jit(solution)/shard_map/reduce_scatter | solution.py:84
  7.2 4.8 %collective-permute-start = (s32[2,256]{1,0:T(2,128)}, s32[2,256]{1,0:T(2,128)S(1)}, u32[]{:S(2)}, u32[]{:S(2)}) collective-permute-start(s32[2,256]{1,0:T(2,128)} %bitcast.151), channel_id=1, source_target_pairs={{0,1},{1,0},{2,3},{3,2},{4,5},{5,4},{6,7},{7,6},{8,9},{9,8},{10,11... | collective-permute-start | bytes 6152 | tf_op jit(solution)/shard_map/ppermute | solution.py:63
  10.3 6.6 %collective-permute-start.1 = (bf16[256,384]{1,0:T(8,128)(2,1)}, bf16[256,384]{1,0:T(8,128)(2,1)S(1)}, u32[]{:S(2)}, u32[]{:S(2)}) collective-permute-start(bf16[256,384]{1,0:T(8,128)(2,1)} %param.9), channel_id=1, source_target_pairs={{0,1},{1,0},{2,3},{3,2},{4,5},{5,4},{6,7},{7,6},{8,9},{9,8},{10,11... | collective-permute-start | bytes 589832 | tf_op jit(solution)/shard_map/ppermute | solution.py:63
  19.7 6.0 %slice-start = ((s8[6291456]{0:T(1024)(128)(4,1)}), s8[4194304]{0:T(1024)(128)(4,1)S(1)}, s32[]{:S(2)}) async-start(s8[6291456]{0:T(1024)(128)(4,1)} %bitcast.141), calls=%async_computation.2 | async-start | bytes 8388608
  19.8 6.0 %slice-start.1 = ((s8[6291456]{0:T(1024)(128)(4,1)}), s8[2097152]{0:T(1024)(128)(4,1)S(1)}, s32[]{:S(2)}) async-start(s8[6291456]{0:T(1024)(128)(4,1)} %bitcast.141), calls=%async_computation.3 | async-start | bytes 4194304
  25.7 2.9 %copy-start.2 = (f32[1,32,224]{2,1,0:T(8,128)S(1)}, f32[1,32,224]{2,1,0:T(8,128)}, u32[]{:S(2)}) copy-start(f32[1,32,224]{2,1,0:T(8,128)} %param.15) | copy-start | bytes 86020
  25.7 8.2 %copy-start.1 = (bf16[256,384]{1,0:T(8,128)(2,1)S(1)}, bf16[256,384]{1,0:T(8,128)(2,1)}, u32[]{:S(2)}) copy-start(bf16[256,384]{1,0:T(8,128)(2,1)} %param.9) | copy-start | bytes 589828
  28.1 5.7 %collective-permute-start.2 = (bf16[256,384]{1,0:T(8,128)(2,1)S(1)}, bf16[256,384]{1,0:T(8,128)(2,1)S(1)}, u32[]{:S(2)}, u32[]{:S(2)}) collective-permute-start(bf16[256,384]{1,0:T(8,128)(2,1)S(1)} %fusion.35), channel_id=1, source_target_pairs={{0,1},{1,0},{2,3},{3,2},{4,5},{5,4},{6,7},{7,6},{8,9},{9,8},{10,11... | collective-permute-start | bytes 589832 | tf_op jit(solution)/shard_map/ppermute | solution.py:68
  36.0 5.7 %collective-permute-start.3 = (bf16[256,384]{1,0:T(8,128)(2,1)S(1)}, bf16[256,384]{1,0:T(8,128)(2,1)S(1)}, u32[]{:S(2)}, u32[]{:S(2)}) collective-permute-start(bf16[256,384]{1,0:T(8,128)(2,1)S(1)} %get-tuple-element.17), channel_id=1, source_target_pairs={{0,1},{1,0},{2,3},{3,2},{4,5},{5,4},{6,7},{7,6},{8,9},{9,8},{10,11... | collective-permute-start | bytes 589832 | tf_op jit(solution)/shard_map/ppermute | solution.py:63
  47.9 9.9 %copy-start.3 = (bf16[384,8]{0,1:T(8,128)(2,1)S(1)}, bf16[384,8]{0,1:T(8,128)(2,1)}, u32[]{:S(2)}) copy-start(bf16[384,8]{0,1:T(8,128)(2,1)} %param.11) | copy-start | bytes 18436
  58.3 5.7 %collective-permute-start.4 = (bf16[256,384]{1,0:T(8,128)(2,1)S(1)}, bf16[256,384]{1,0:T(8,128)(2,1)S(1)}, u32[]{:S(2)}, u32[]{:S(2)}) collective-permute-start(bf16[256,384]{1,0:T(8,128)(2,1)S(1)} %fusion.36), channel_id=1, source_target_pairs={{0,1},{1,0},{2,3},{3,2},{4,5},{5,4},{6,7},{7,6},{8,9},{9,8},{10,11... | collective-permute-start | bytes 589832 | tf_op jit(solution)/shard_map/ppermute | solution.py:68
Sparse Core Ops, SparseCore 0:
  47.4 85.4 reduce-scatter.1
